TPU v7x, 32 devices: a whole 2x2x4 slice. The times are simulated.
32 devices in a mesh: group: 2 (over y), tile: 4 (over x, core), seq: 4 (over z).
Axes of the slice: x: 2, y: 2, z: 4, core: 2. Of those that a mesh axis runs over, the one named last changes fastest.
Arguments:
- hidden: bfloat16 [8, 1024, 3072], P(('group', 'tile'), 'seq'), parts along dimension 0
- modulation: float32 [10, 3072], P('group'), parts along dimension 0, may hold values from -3 to 3
- w_qkv: bfloat16 [3072, 9216], P('tile', 'seq')
- w_out: bfloat16 [3072, 3072], P('seq', 'tile'), may hold values from -0.109375 to 0.109375
- w_head: bfloat16 [3072, 64], replicated, may hold values from -0.109375 to 0.109375
- latent: float32 [8, 1024, 64], P(('group', 'tile'), 'seq'), parts along dimension 0, may hold values from -6 to 6
- weights_int: int32 [8, 1024], P(('group', 'tile'), 'seq'), parts along dimension 0, may hold values from 1 to 8
- step_index: int32 [2], P('group'), parts along dimension 0, may hold values from 0 to 13
Outputs:
- stepped: float32 [8, 1024, 64], P(('group', 'tile'), 'seq'), parts along dimension 0
- clean: float32 [8, 1024, 64], P(('group', 'tile'), 'seq'), parts along dimension 0
There are 2 independent parts, one for each index of `group`. A program takes and returns all parts, laid end to end along the dimension named above; an argument that names none is the same for every part. Nothing has to cross between parts.
All inputs are finite; a program needn't handle non-finite values.
Results may differ from a plain program's by a relative error of at most 0.0055.
Values may be sent and summed in bfloat16 or wider, within the bound.
A program may use at most 64 MiB of HBM per device.

v0:
```python
import math

import jax
import jax.numpy as jnp
from jax import lax
from jax.sharding import PartitionSpec as P

HD = 128
NSTEPS = 28


def shifted(value, axis, steps):
    count = lax.axis_size(axis)
    leading, last = (max(0, -steps), min(count, count - steps))
    return lax.ppermute(value, axis, [(source, source + steps) for source in range(leading, last)])


def layer_norm(values):
    mean = jnp.mean(values, axis=-1, keepdims=True)
    centred = values - mean
    spread = jnp.mean(centred * centred, axis=-1, keepdims=True)
    return centred * lax.rsqrt(spread + 1e-06)


def root_norm(values):
    return values * lax.rsqrt(jnp.mean(values * values, axis=-1, keepdims=True) + 1e-06)


def noise_level(index, steps):
    level = 1.0 - index / steps
    return 3.0 * level / (1.0 + 2.0 * level)


def shards(hidden, modulation, w_qkv, w_out, w_head, latent, weights_int, step_index):
    local = hidden[0].astype(jnp.float32)
    norm_in = (layer_norm(local) * (1.0 + modulation[1]) + modulation[0]).astype(jnp.bfloat16)
    gathered = lax.all_gather(norm_in, "seq", axis=0, tiled=True)
    length = gathered.shape[0]
    heads_here = w_qkv.shape[1] // (3 * HD)
    projected = jnp.dot(
        gathered,
        lax.all_gather(w_qkv, "tile", axis=0, tiled=True),
        preferred_element_type=jnp.float32,
    )
    full_out = lax.all_gather(w_out, "tile", axis=1, tiled=True)
    projected = projected.reshape(length, heads_here, 3, HD)
    queries = root_norm(projected[:, :, 0]).astype(jnp.bfloat16)
    keys = root_norm(projected[:, :, 1]).astype(jnp.bfloat16)
    values = projected[:, :, 2].astype(jnp.bfloat16)
    block = min(512, length)
    scale = 1.0 / math.sqrt(HD)
    pieces = []
    for first in range(0, length, block):
        scores = (
            jnp.einsum(
                "qhe,khe->hqk",
                queries[first : first + block],
                keys,
                preferred_element_type=jnp.float32,
            )
            * scale
        )
        expo = jnp.exp(scores)
        probs = (expo / jnp.sum(expo, axis=-1, keepdims=True)).astype(jnp.bfloat16)
        pieces.append(
            jnp.einsum("hqk,khe->qhe", probs, values, preferred_element_type=jnp.float32).astype(
                jnp.bfloat16
            )
        )
    attended = jnp.concatenate(pieces, axis=0).reshape(length, heads_here * HD)
    summed = lax.psum_scatter(
        jnp.dot(attended, full_out, preferred_element_type=jnp.float32).astype(jnp.bfloat16),
        "seq",
        scatter_dimension=0,
        tiled=True,
    ).astype(jnp.float32)
    mixed = local + modulation[2] * summed
    norm_out = (layer_norm(mixed) * (1.0 + modulation[4]) + modulation[3]).astype(jnp.bfloat16)
    velocity = jnp.dot(norm_out, w_head, preferred_element_type=jnp.float32)
    index = step_index[0].astype(jnp.float32)
    now = noise_level(index, NSTEPS)
    after = noise_level(index + 1.0, NSTEPS)
    base = latent[0]
    weight = weights_int[0].astype(jnp.float32)
    moved = base + (after - now) * velocity
    guess = base - now * velocity
    weighted = jnp.concatenate([moved, guess], axis=1) * weight[:, None]
    seq_count = lax.axis_size("seq")
    place = lax.axis_index("seq")
    prev_tile = (
        shifted(weighted.astype(jnp.bfloat16), "tile", 1).astype(weighted.dtype),
        shifted(weight.astype(jnp.bfloat16), "tile", 1).astype(weight.dtype),
    )
    prev_sums, prev_weight = (
        shifted(prev_tile[0].astype(jnp.bfloat16), "seq", -(seq_count - 2)).astype(jnp.float32),
        shifted(prev_tile[1].astype(jnp.bfloat16), "seq", -(seq_count - 2)).astype(jnp.float32),
    )
    next_tile = (
        shifted(weighted.astype(jnp.bfloat16), "tile", -1).astype(weighted.dtype),
        shifted(weight.astype(jnp.bfloat16), "tile", -1).astype(weight.dtype),
    )
    next_sums, next_weight = (
        shifted(next_tile[0].astype(jnp.bfloat16), "seq", seq_count - 2).astype(jnp.float32),
        shifted(next_tile[1].astype(jnp.bfloat16), "seq", seq_count - 2).astype(jnp.float32),
    )
    take_prev = place < 2
    take_next = place >= seq_count - 2
    totals = weighted + jnp.where(take_prev, prev_sums, 0.0) + jnp.where(take_next, next_sums, 0.0)
    norms = weight + jnp.where(take_prev, prev_weight, 0.0) + jnp.where(take_next, next_weight, 0.0)
    joined = totals / norms[:, None]
    channels = velocity.shape[1]
    return (joined[None, :, :channels], joined[None, :, channels:])


def solution(mesh):
    in_specs = (
        P(("group", "tile"), "seq", None),
        P("group", None),
        P("tile", "seq"),
        P("seq", "tile"),
        P(),
        P(("group", "tile"), "seq", None),
        P(("group", "tile"), "seq"),
        P("group"),
    )
    out_specs = (P(("group", "tile"), "seq", None), P(("group", "tile"), "seq", None))
    return jax.shard_map(shards, mesh=mesh, in_specs=in_specs, out_specs=out_specs, check_vma=False)
```

profile of v0, /device:TPU:2, one launch (start us, length us, event | category | flops | bytes accessed | tf_op | source)
XLA Modules:
  0.0 436.0 jit_solution(16859526870282650366)
XLA Ops:
  7.2 0.0 copy-start
  7.2 0.0 copy-start.1
  7.2 0.0 all-gather.4.cloned.1.call-start
  7.2 1.9 fusion.30
  9.1 1.7 convert_reduce_fusion
  10.8 2.0 fusion.8
  12.8 1.9 fusion.11
  14.7 0.0 all-gather.4.cloned.1.call-update
  14.8 0.0 all-gather.6.cloned.1.call-start
  14.8 0.7 all-gather.6.cloned.1.call-update
  15.5 0.0 all-gather.8.cloned.1.call-start
  15.6 0.7 all-gather.8.cloned.1.call-update
  16.3 0.0 reduce-scatter.2.cloned.1.call-start
  16.3 115.2 %all-gather.4.cloned.1.call-done = bf16[1024,3072]{1,0:T(8,128)(2,1)} async-done(((bf16[256,3072]{1,0:T(8,128)(2,1)}), bf16[1024,3072]{1,0:T(8,128)(2,1)}) %all-gather.4.cloned.1.call-update) | async-done | bytes 6291472 | tf_op jit(solution)/shard_map/all_gather | solution.py:37
  131.5 89.7 %all-gather.6.cloned.1.call-done = bf16[3072,2304]{1,0:T(8,128)(2,1)} async-done(((bf16[768,2304]{1,0:T(8,128)(2,1)}), bf16[3072,2304]{1,0:T(8,128)(2,1)}) %all-gather.6.cloned.1.call-update) | async-done | bytes 14155792 | tf_op jit(solution)/shard_map/all_gather | solution.py:42
  221.1 19.6 %fusion.31 = f32[1024,2304]{0,1:T(8,128)S(1)} fusion(bf16[1024,3072]{1,0:T(8,128)(2,1)} %all-gather.4.cloned.1.call-done, bf16[3072,2304]{1,0:T(8,128)(2,1)} %all-gather.6.cloned.1.call-done), kind=kOutput, calls=%fused_computation.60 | convolution fusion | flops 14495514624 | bytes 29884416 | tf_op jit(solution)/shard_map/dot_general | solution.py:40
  240.7 3.5 copy-done.3
  244.3 2.0 slice.50
  246.3 3.6 copy.21
  249.9 2.9 fusion.12
  252.9 2.3 multiply_reduce_fusion.1
  255.2 0.0 slice-start
  255.2 1.0 fusion.13
  256.2 0.0 slice-start.1
  256.2 8.2 %fusion = (f32[6,512]{1,0:T(8,128)S(1)}, f32[6,512,1024]{2,1,0:T(8,128)}) fusion(f32[1024,6,3,128]{0,3,2,1:T(8,128)} %bitcast.78, f32[1024,6]{0,1:T(8,128)S(1)} %add_rsqrt_fusion, bf16[1024,6,128]{2,0,1:T(8,128)(2,1)S(1)} %fusion.13), kind=kOutput, calls=%fused_computation.4 | convolution fusion | flops 813167616 | bytes 16560128 | tf_op jit(solution)/shard_map/qhe,khe->hqk/dot_general | solution.py:55
  264.5 2.7 fusion.1
  267.2 6.0 %fusion.19 = bf16[512,6,128]{0,2,1:T(8,128)(2,1)S(1)} fusion(f32[6,512,1024]{2,1,0:T(8,128)} %get-tuple-element.14, f32[6,512]{1,0:T(8,128)S(1)} %get-tuple-element.13, f32[1024,6,3,128]{0,3,2,1:T(8,128)S(1)} %bitcast.82), kind=kOutput, calls=%fused_computation.35 | convolution fusion | flops 815136768 | bytes 14958592 | tf_op jit(solution)/shard_map/hqk,khe->qhe/dot_general | solution.py:66
  273.2 2.9 fusion.20
  276.1 0.2 pad_maximum_fusion
  276.3 0.0 all-gather.8.cloned.1.call-done
  276.3 9.5 %convolution_convert_fusion = bf16[1024,3072]{1,0:T(8,128)(2,1)} fusion(bf16[1024,768]{0,1:T(8,128)(2,1)S(1)} %bitcast.84, bf16[768,3072]{1,0:T(8,128)(2,1)} %all-gather.8.cloned.1.call-done), kind=kOutput, calls=%fused_computation.8 | convolution fusion | flops 4834983936 | bytes 12582912 | tf_op jit(solution)/shard_map/dot_general | solution.py:72
  285.9 0.0 reduce-scatter.2.cloned.1.call-update
  286.7 111.3 %reduce-scatter.2.cloned.1.call-done = bf16[256,3072]{1,0:T(8,128)(2,1)} async-done(((bf16[1024,3072]{1,0:T(8,128)(2,1)}), bf16[256,3072]{1,0:T(8,128)(2,1)}) %reduce-scatter.2.cloned.1.call-update) | async-done | bytes 1572880 | tf_op jit(solution)/shard_map/reduce_scatter | solution.py:71
  398.0 2.1 fusion.14
  400.2 0.8 multiply_reduce_fusion
  401.0 1.1 bitcast_add_fusion
  402.1 1.9 collective-permute-start
  404.1 3.6 collective-permute-start.2
  407.7 1.9 collective-permute-start.4
  409.6 3.6 collective-permute-start.6
  413.3 1.3 collective-permute-start.5
  414.6 0.0 collective-permute-done.6
  414.6 5.4 %collective-permute-start.7 = (bf16[256]{0:T(256)(128)(2,1)S(1)}, bf16[256]{0:T(256)(128)(2,1)S(1)}, u32[]{:S(2)}, u32[]{:S(2)}) collective-permute-start(bf16[256]{0:T(256)(128)(2,1)S(1)} %collective-permute-done.6), channel_id=1, source_target_pairs={{0,2},{1,3},{4,6},{5,7},{8,10},{9,11},{12,14},{13,15},{16,18},{17,... | collective-permute-start | bytes 1544 | tf_op jit(solution)/shard_map/ppermute | solution.py:15
  420.1 1.3 collective-permute-start.1
  421.4 5.4 %collective-permute-start.3 = (bf16[256,128]{0,1:T(8,128)(2,1)S(1)}, bf16[256,128]{0,1:T(8,128)(2,1)S(1)}, u32[]{:S(2)}, u32[]{:S(2)}) collective-permute-start(bf16[256,128]{0,1:T(8,128)(2,1)S(1)} %collective-permute-done.2), channel_id=1, source_target_pairs={{0,2},{1,3},{4,6},{5,7},{8,10},{9,11},{12,14},{13,15},{16,18},{17,... | collective-permute-start | bytes 196616 | tf_op jit(solution)/shard_map/ppermute | solution.py:15
  426.9 0.3 collective-permute-done.1
  427.1 1.6 collective-permute-done.3
  428.8 0.7 slice_bitcast_fusion.1
  (36 shorter events, 0.2 us)
Async XLA Ops:
  7.2 393.8 %copy-start = (bf16[3072,64]{0,1:T(8,128)(2,1)S(1)}, bf16[3072,64]{0,1:T(8,128)(2,1)}, u32[]{:S(2)}) copy-start(bf16[3072,64]{0,1:T(8,128)(2,1)} %param.12) | copy-start | bytes 1179652
  7.2 5.6 %copy-start.1 = (bf16[1,256,3072]{2,1,0:T(8,128)(2,1)S(1)}, bf16[1,256,3072]{2,1,0:T(8,128)(2,1)}, u32[]{:S(2)}) copy-start(bf16[1,256,3072]{2,1,0:T(8,128)(2,1)} %param.8) | copy-start | bytes 4718596
  7.2 124.3 %all-gather.4.cloned.1.call-start = ((), (), s32[]{:S(2)}) async-start(), calls=%async_computation.1 | async-start | bytes 7864320 | tf_op jit(solution)/shard_map/all_gather | solution.py:37
  14.8 206.4 %all-gather.6.cloned.1.call-start = ((), (), s32[]{:S(2)}) async-start(), calls=%async_computation.2 | async-start | bytes 17694720 | tf_op jit(solution)/shard_map/all_gather | solution.py:42
  15.5 260.8 %all-gather.8.cloned.1.call-start = ((), (), s32[]{:S(2)}) async-start(), calls=%async_computation.3 | async-start | bytes 5898240 | tf_op jit(solution)/shard_map/all_gather | solution.py:45
  16.3 381.8 %reduce-scatter.2.cloned.1.call-start = ((), (), s32[]{:S(2)}) async-start(), calls=%async_computation.4 | async-start | bytes 7864320 | tf_op jit(solution)/shard_map/reduce_scatter | solution.py:71
  240.7 3.6 copy-start.3
  249.9 5.3 %copy-start.2 = (f32[1024,6,1,128]{3,0,1,2:T(8,128)S(1)}, f32[1024,6,1,128]{3,0,1,2:T(8,128)}, u32[]{:S(2)}) copy-start(f32[1024,6,1,128]{3,0,1,2:T(8,128)} %copy.21) | copy-start | bytes 9437188
  255.2 9.2 %slice-start = ((s8[9437184]{0:T(1024)(128)(4,1)}), s8[4194304]{0:T(1024)(128)(4,1)S(1)}, s32[]{:S(2)}) async-start(s8[9437184]{0:T(1024)(128)(4,1)} %bitcast.79), calls=%async_computation.5 | async-start | bytes 8388608
  256.2 8.3 %slice-start.1 = ((s8[9437184]{0:T(1024)(128)(4,1)}), s8[4194304]{0:T(1024)(128)(4,1)S(1)}, s32[]{:S(2)}) async-start(s8[9437184]{0:T(1024)(128)(4,1)} %bitcast.79), calls=%async_computation.6 | async-start | bytes 8388608
  256.2 8.2 %slice-start.2 = ((s8[9437184]{0:T(1024)(128)(4,1)}), s8[1048576]{0:T(1024)(128)(4,1)S(1)}, s32[]{:S(2)}) async-start(s8[9437184]{0:T(1024)(128)(4,1)} %bitcast.79), calls=%async_computation.7 | async-start | bytes 2097152
  285.9 0.7 copy-start.7
  398.0 2.1 copy-start.4
  398.0 3.0 copy-start.5
  398.0 3.0 copy-start.6
  398.0 3.0 copy-start.8
  402.1 17.9 %collective-permute-start = (bf16[256,128]{0,1:T(8,128)(2,1)S(1)}, bf16[256,128]{0,1:T(8,128)(2,1)S(1)}, u32[]{:S(2)}, u32[]{:S(2)}) collective-permute-start(bf16[256,128]{0,1:T(8,128)(2,1)S(1)} %fusion.27), channel_id=1, source_target_pairs={{0,4},{4,8},{8,12},{1,5},{5,9},{9,13},{2,6},{6,10},{10,14},{3,7},{... | collective-permute-start | bytes 196616 | tf_op jit(solution)/shard_map/ppermute | solution.py:15
  404.1 17.3 %collective-permute-start.2 = (bf16[256,128]{0,1:T(8,128)(2,1)S(1)}, bf16[256,128]{0,1:T(8,128)(2,1)S(1)}, u32[]{:S(2)}, u32[]{:S(2)}) collective-permute-start(bf16[256,128]{0,1:T(8,128)(2,1)S(1)} %fusion.27), channel_id=1, source_target_pairs={{4,0},{8,4},{12,8},{5,1},{9,5},{13,9},{6,2},{10,6},{14,10},{7,3},{... | collective-permute-start | bytes 196616 | tf_op jit(solution)/shard_map/ppermute | solution.py:15
  407.7 5.6 %collective-permute-start.4 = (bf16[256]{0:T(256)(128)(2,1)S(1)}, bf16[256]{0:T(256)(128)(2,1)S(1)}, u32[]{:S(2)}, u32[]{:S(2)}) collective-permute-start(bf16[256]{0:T(256)(128)(2,1)S(1)} %convert_element_type.109), channel_id=1, source_target_pairs={{0,4},{4,8},{8,12},{1,5},{5,9},{9,13},{2,6},{6,10},{10,14},{3,7},{... | collective-permute-start | bytes 1544 | tf_op jit(solution)/shard_map/ppermute | solution.py:15
  409.6 5.0 %collective-permute-start.6 = (bf16[256]{0:T(256)(128)(2,1)S(1)}, bf16[256]{0:T(256)(128)(2,1)S(1)}, u32[]{:S(2)}, u32[]{:S(2)}) collective-permute-start(bf16[256]{0:T(256)(128)(2,1)S(1)} %convert_element_type.109), channel_id=1, source_target_pairs={{4,0},{8,4},{12,8},{5,1},{9,5},{13,9},{6,2},{10,6},{14,10},{7,3},{... | collective-permute-start | bytes 1544 | tf_op jit(solution)/shard_map/ppermute | solution.py:15
  413.3 13.5 %collective-permute-start.5 = (bf16[256]{0:T(256)(128)(2,1)S(1)}, bf16[256]{0:T(256)(128)(2,1)S(1)}, u32[]{:S(2)}, u32[]{:S(2)}) collective-permute-start(bf16[256]{0:T(256)(128)(2,1)S(1)} %collective-permute-done.4), channel_id=1, source_target_pairs={{2,0},{3,1},{6,4},{7,5},{10,8},{11,9},{14,12},{15,13},{18,16},{19,... | collective-permute-start | bytes 1544 | tf_op jit(solution)/shard_map/ppermute | solution.py:15
  414.6 12.2 %collective-permute-start.7 = (bf16[256]{0:T(256)(128)(2,1)S(1)}, bf16[256]{0:T(256)(128)(2,1)S(1)}, u32[]{:S(2)}, u32[]{:S(2)}) collective-permute-start(bf16[256]{0:T(256)(128)(2,1)S(1)} %collective-permute-done.6), channel_id=1, source_target_pairs={{0,2},{1,3},{4,6},{5,7},{8,10},{9,11},{12,14},{13,15},{16,18},{17,... | collective-permute-start | bytes 1544 | tf_op jit(solution)/shard_map/ppermute | solution.py:15
  420.1 7.1 %collective-permute-start.1 = (bf16[256,128]{0,1:T(8,128)(2,1)S(1)}, bf16[256,128]{0,1:T(8,128)(2,1)S(1)}, u32[]{:S(2)}, u32[]{:S(2)}) collective-permute-start(bf16[256,128]{0,1:T(8,128)(2,1)S(1)} %collective-permute-done), channel_id=1, source_target_pairs={{2,0},{3,1},{6,4},{7,5},{10,8},{11,9},{14,12},{15,13},{18,16},{19,... | collective-permute-start | bytes 196616 | tf_op jit(solution)/shard_map/ppermute | solution.py:15
  421.4 7.3 %collective-permute-start.3 = (bf16[256,128]{0,1:T(8,128)(2,1)S(1)}, bf16[256,128]{0,1:T(8,128)(2,1)S(1)}, u32[]{:S(2)}, u32[]{:S(2)}) collective-permute-start(bf16[256,128]{0,1:T(8,128)(2,1)S(1)} %collective-permute-done.2), channel_id=1, source_target_pairs={{0,2},{1,3},{4,6},{5,7},{8,10},{9,11},{12,14},{13,15},{16,18},{17,... | collective-permute-start | bytes 196616 | tf_op jit(solution)/shard_map/ppermute | solution.py:15
Sparse Core Ops, SparseCore 0:
  14.9 116.5 all-gather.3
  133.0 88.0 all-gather.5
  222.7 37.4 all-gather.7
  286.0 111.9 reduce-scatter.1
where the time goes:
time: 438 us; the launch traced here: 436 us
  waiting for transfers between devices  319 us (73%)
  matrix products  50 us (11%)
  starting transfers between devices  24.8 us (6%)
  other arithmetic  16.9 us (4%)
  between operations  14.9 us (3%)
  local copies, waits for them, and re-layouts  9.9 us (2%)
    all_gather x1, waiting for transfers between devices, shards(): gathered = lax.all_gather(norm_in, 'seq', axis=0, tiled=True)  115 us
    reduce_scatter x1, waiting for transfers between devices, shards(): lax.psum_scatter(jnp.dot(attended, full_out, preferred_element_type=jnp.f...  111 us
    all_gather x1, waiting for transfers between devices, shards(): lax.all_gather(w_qkv, 'tile', axis=0, tiled=True)  89.7 us
    ppermute x8, starting transfers between devices, shifted(): lax.ppermute(value, axis, [(source, source + steps) for source in range(l...  24.6 us
    dot_general x1, matrix products, shards(): jnp.dot(gathered, lax.all_gather(w_qkv, 'tile', axis=0, tiled=True), pref...  19.6 us
    dot_general x2, matrix products, shards(): jnp.einsum('qhe,khe->hqk', queries[first:first + block], keys, preferred_...  10.9 us
    dot_general x1, matrix products, shards(): jnp.dot(attended, full_out, preferred_element_type=jnp.float32)  9.54 us
    dot_general x2, matrix products, shards(): jnp.einsum('hqk,khe->qhe', probs, values, preferred_element_type=jnp.floa...  8.92 us
  transfers between devices with their start and end apart: 12, of which 5 were waited for; matrix products, arithmetic and copies ran while one was open for 12% of the time, Pallas kernels for 0%

commit v1 on v0

v1 whole, which is shorter than its diff:
```python
import functools
import math

import jax
import jax.numpy as jnp
from jax import lax
from jax.experimental import pallas as pl
from jax.experimental.pallas import tpu as pltpu
from jax.sharding import PartitionSpec as P

HD = 128
NSTEPS = 28


def layer_norm(values):
    mean = jnp.mean(values, axis=-1, keepdims=True)
    centred = values - mean
    spread = jnp.mean(centred * centred, axis=-1, keepdims=True)
    return centred * lax.rsqrt(spread + 1e-06)


def root_norm(values):
    return values * lax.rsqrt(jnp.mean(values * values, axis=-1, keepdims=True) + 1e-06)


def noise_level(index, steps):
    level = 1.0 - index / steps
    return 3.0 * level / (1.0 + 2.0 * level)


MESH = pl.DeviceIdType.MESH


def run(cond, body):
    if cond is None:
        body()
    else:
        pl.when(cond)(body)


def arrives(place, count, way, far):
    return place >= far if way == 0 else place <= count - 1 - far


def goes_on(place, count, way):
    return place < count - 1 if way == 0 else place > 0


def gather_kernel(
    groups, chips, seqs, norm, wq, wo, n_all, q_all, o_all, v_norm, v_wq, v_wo, local,
    nz_s, nz_r, oz_s, oz_r, qx_s, qx_r, ox_s, ox_r, qy_s, qy_r, oy_s, oy_r, qc_s, qc_r, oc_s, oc_r,
):
    group, tile, place = lax.axis_index("group"), lax.axis_index("tile"), lax.axis_index("seq")
    chip, core = tile // 2, tile % 2
    other = 1 - core
    partner = {"tile": chip * 2 + other}
    q_rows, o_rows = wq.shape[0] // groups, wo.shape[0] // groups
    both = jnp.logical_and

    def q_part(owner, part):
        return q_all.at[owner, pl.ds(pl.multiple_of(part * q_rows, 8), q_rows)]

    def o_part(owner, row, part):
        return o_all.at[owner, row, pl.ds(pl.multiple_of(part * o_rows, 8), o_rows)]

    def along_seq(way):
        return {"seq": place + 1 - 2 * way}

    def along_chip(way):
        return {"tile": tile + 2 - 4 * way}

    def peer(step):
        return {"group": (group + step) % groups}

    barrier = pltpu.get_barrier_semaphore()
    greet = [(goes_on(place, seqs, way), along_seq(way)) for way in (0, 1)]
    greet += [(goes_on(chip, chips, way), along_chip(way)) for way in (0, 1)]
    greet += [(None, peer(step)) for step in range(1, groups)] + [(None, partner)]
    for cond, device in greet:
        run(cond, lambda device=device: pl.semaphore_signal(barrier, inc=1, device_id=device, device_id_type=MESH))
    met = groups + sum(goes_on(at, count, way).astype(jnp.int32) for at, count in ((place, seqs), (chip, chips)) for way in (0, 1))
    pl.semaphore_wait(barrier, met)

    sent = []

    def copy(source, target, send, recv, device):
        return pltpu.make_async_remote_copy(
            src_ref=source, dst_ref=target, send_sem=send, recv_sem=recv, device_id=device, device_id_type=MESH
        )

    def start(cond, *made):
        run(cond, lambda: copy(*made).start())
        sent.append((cond, made))

    def arrived(cond, target, send, recv, device):
        run(cond, lambda: copy(target, target, send, recv, device).wait_recv())

    def q_to_peers(cond, at, source):
        for step in range(1, groups):
            start(cond, source, q_part(at * 2 + core, group), qy_s.at[at, step], qy_r.at[at, step], peer(step))

    def q_to_partner(cond, at, part, source):
        start(cond, source, q_part(at * 2 + core, part), qc_s.at[at, part], qc_r.at[at, part], partner)

    def o_to_peers(cond, at, row, source):
        for step in range(1, groups):
            start(cond, source, o_part(at * 2 + core, row, group), oy_s.at[at, row, step], oy_r.at[at, row, step], peer(step))

    def o_to_partner(cond, at, row, part, source):
        start(cond, source, o_part(at * 2 + core, row, part), oc_s.at[at, row, part], oc_r.at[at, row, part], partner)

    def o_along_chip(cond, way, far, at, row, source):
        start(cond, source, o_part(at * 2 + core, row, group), ox_s.at[way, far, row], ox_r.at[way, far, row], along_chip(way))

    loads = [pltpu.make_async_copy(a, b, local.at[k]) for k, (a, b) in enumerate(((norm, v_norm), (wq, v_wq), (wo, v_wo)))]
    for load in loads:
        load.start()

    own_q = wq.at[pl.ds(pl.multiple_of(group * q_rows, 8), q_rows)]
    own_o = wo.at[pl.ds(pl.multiple_of(group * o_rows, 8), o_rows)]
    for way in (0, 1):
        go = goes_on(place, seqs, way)
        start(go, own_o, o_part(tile, place, group), oz_s.at[way, 1], oz_r.at[way, 1], along_seq(way))
        start(go, norm, n_all.at[place], nz_s.at[way, 1], nz_r.at[way, 1], along_seq(way))
        go = goes_on(chip, chips, way)
        start(go, own_q, q_part(tile, group), qx_s.at[way, 1], qx_r.at[way, 1], along_chip(way))
        o_along_chip(go, way, 1, chip, place, own_o)
    for part in range(groups):
        q_to_partner(None, chip, part, wq.at[pl.ds(part * q_rows, q_rows)])
        o_to_partner(None, chip, place, part, wo.at[pl.ds(part * o_rows, o_rows)])

    stores = [pltpu.make_async_copy(b, a, local.at[k]) for k, (a, b) in enumerate(((n_all.at[place], v_norm), (q_all.at[tile], v_wq), (o_all.at[tile, place], v_wo)))]
    for load in loads:
        load.wait()
    for store in stores:
        store.start()

    def seq_step(far):
        for way in (0, 1):
            here = arrives(place, seqs, way, far)
            row = place - far if way == 0 else place + far
            piece = o_part(tile, row, group)
            arrived(here, piece, oz_s.at[way, far], oz_r.at[way, far], along_seq(way))
            if far < seqs - 1:
                start(both(here, goes_on(place, seqs, way)), piece, piece, oz_s.at[way, far + 1], oz_r.at[way, far + 1], along_seq(way))
            for side in (0, 1):
                o_along_chip(both(here, goes_on(chip, chips, side)), side, 1, chip, row, piece)
            o_to_peers(here, chip, row, piece)
            o_to_partner(here, chip, row, group, piece)
        for way in (0, 1):
            here = arrives(place, seqs, way, far)
            row = place - far if way == 0 else place + far
            piece = n_all.at[row]
            arrived(here, piece, nz_s.at[way, far], nz_r.at[way, far], along_seq(way))
            if far < seqs - 1:
                start(both(here, goes_on(place, seqs, way)), piece, piece, nz_s.at[way, far + 1], nz_r.at[way, far + 1], along_seq(way))

    def chip_step(far):
        for way in (0, 1):
            here = arrives(chip, chips, way, far)
            at = chip - far if way == 0 else chip + far
            piece = q_part(at * 2 + core, group)
            arrived(here, piece, qx_s.at[way, far], qx_r.at[way, far], along_chip(way))
            if far < chips - 1:
                start(both(here, goes_on(chip, chips, way)), piece, piece, qx_s.at[way, far + 1], qx_r.at[way, far + 1], along_chip(way))
            q_to_peers(here, at, piece)
            q_to_partner(here, at, group, piece)

    for far in range(1, max(chips, seqs)):
        if far < seqs:
            seq_step(far)
        if far < chips:
            chip_step(far)

    for far in range(1, chips):
        for way in (0, 1):
            here = arrives(chip, chips, way, far)
            at = chip - far if way == 0 else chip + far

            for row in range(seqs):
                piece = o_part(at * 2 + core, row, group)
                arrived(here, piece, ox_s.at[way, far, row], ox_r.at[way, far, row], along_chip(way))
                if far < chips - 1:
                    o_along_chip(both(here, goes_on(chip, chips, way)), way, far + 1, at, row, piece)
                o_to_peers(here, at, row, piece)
                o_to_partner(here, at, row, group, piece)

    for step in range(1, groups):
        part = (group + groups - step) % groups
        for at in range(chips):
            away = chip != at
            piece = q_part(at * 2 + core, part)
            arrived(away, piece, qy_s.at[at, step], qy_r.at[at, step], partner)
            q_to_partner(away, at, part, piece)
        for at in range(chips):
            for row in range(seqs):
                away = jnp.logical_or(chip != at, place != row)
                piece = o_part(at * 2 + core, row, part)
                arrived(away, piece, oy_s.at[at, row, step], oy_r.at[at, row, step], partner)
                o_to_partner(away, at, row, part, piece)

    for at in range(chips):
        for part in range(groups):
            arrived(None, q_part(at * 2 + other, part), qc_s.at[at, part], qc_r.at[at, part], partner)
            for row in range(seqs):
                arrived(None, o_part(at * 2 + other, row, part), oc_s.at[at, row, part], oc_r.at[at, row, part], partner)
    for cond, made in sent:
        run(cond, lambda made=made: copy(*made).wait_send())
    for store in stores:
        store.wait()


def gather(norm, wq, wo):
    groups, tiles, seqs = (lax.axis_size(name) for name in ("group", "tile", "seq"))
    chips = tiles // 2
    pairs = [(2, seqs), (2, seqs), (2, chips), (2, chips, seqs), (chips, groups), (chips, seqs, groups), (chips, groups), (chips, seqs, groups)]
    return pl.pallas_call(
        functools.partial(gather_kernel, groups, chips, seqs),
        out_shape=(
            jax.ShapeDtypeStruct((seqs,) + norm.shape, norm.dtype),
            jax.ShapeDtypeStruct((tiles,) + wq.shape, wq.dtype),
            jax.ShapeDtypeStruct((tiles, seqs) + wo.shape, wo.dtype),
        ),
        in_specs=[pl.BlockSpec(memory_space=pl.ANY)] * 3,
        out_specs=(pl.BlockSpec(memory_space=pl.ANY),) * 3,
        scratch_shapes=[pltpu.VMEM(a.shape, a.dtype) for a in (norm, wq, wo)]
        + [pltpu.SemaphoreType.DMA((3,))]
        + [pltpu.SemaphoreType.DMA(shape) for shape in pairs for _ in range(2)],
        compiler_params=pltpu.CompilerParams(collective_id=0, has_side_effects=True),
    )(norm, wq, wo)


def shards(hidden, modulation, w_qkv, w_out, w_head, latent, weights_int, step_index):
    local = hidden[0].astype(jnp.float32)
    norm_in = (layer_norm(local) * (1.0 + modulation[1]) + modulation[0]).astype(jnp.bfloat16)
    rows, columns, out_blocks = gather(norm_in, w_qkv, w_out)
    gathered = rows.reshape(-1, rows.shape[2])
    length = gathered.shape[0]
    heads_here = w_qkv.shape[1] // (3 * HD)
    projected = jnp.dot(
        gathered, columns.reshape(-1, columns.shape[2]), preferred_element_type=jnp.float32
    )
    projected = projected.reshape(length, heads_here, 3, HD)
    queries = root_norm(projected[:, :, 0]).astype(jnp.bfloat16)
    keys = root_norm(projected[:, :, 1]).astype(jnp.bfloat16)
    values = projected[:, :, 2].astype(jnp.bfloat16)
    block = min(512, length)
    scale = 1.0 / math.sqrt(HD)
    pieces = []
    for first in range(0, length, block):
        scores = (
            jnp.einsum(
                "qhe,khe->hqk",
                queries[first : first + block],
                keys,
                preferred_element_type=jnp.float32,
            )
            * scale
        )
        expo = jnp.exp(scores)
        probs = (expo / jnp.sum(expo, axis=-1, keepdims=True)).astype(jnp.bfloat16)
        pieces.append(
            jnp.einsum("hqk,khe->qhe", probs, values, preferred_element_type=jnp.float32).astype(
                jnp.bfloat16
            )
        )
    attended = jnp.concatenate(pieces, axis=0).reshape(length, heads_here * HD)
    attended = lax.all_to_all(attended, "seq", split_axis=0, concat_axis=1, tiled=True)
    out_blocks = out_blocks.reshape(out_blocks.shape[0], -1, out_blocks.shape[3])
    summed = jnp.concatenate(
        [
            jnp.dot(attended, out_blocks[at], preferred_element_type=jnp.float32)
            for at in range(out_blocks.shape[0])
        ],
        axis=1,
    )
    mixed = local + modulation[2] * summed
    norm_out = (layer_norm(mixed) * (1.0 + modulation[4]) + modulation[3]).astype(jnp.bfloat16)
    velocity = jnp.dot(norm_out, w_head, preferred_element_type=jnp.float32)
    index = step_index[0].astype(jnp.float32)
    now = noise_level(index, NSTEPS)
    after = noise_level(index + 1.0, NSTEPS)
    base = latent[0]
    weight = weights_int[0].astype(jnp.float32)
    moved = base + (after - now) * velocity
    guess = base - now * velocity
    weighted = jnp.concatenate([moved, guess], axis=1) * weight[:, None]
    seq_count, tile_count = lax.axis_size("seq"), lax.axis_size("tile")
    jump = seq_count - 2
    moves = [
        (t * seq_count + s, (t + 1) * seq_count + s - jump)
        for t in range(tile_count - 1)
        for s in range(jump, seq_count)
    ]
    moves = moves + [(there, here) for here, there in moves]
    other_sums = lax.ppermute(weighted.astype(jnp.bfloat16), ("tile", "seq"), moves)
    other_weight = lax.ppermute(weight.astype(jnp.bfloat16), ("tile", "seq"), moves)
    totals = weighted + other_sums.astype(jnp.float32)
    norms = weight + other_weight.astype(jnp.float32)
    joined = totals / norms[:, None]
    channels = velocity.shape[1]
    return (joined[None, :, :channels], joined[None, :, channels:])


def solution(mesh):
    in_specs = (
        P(("group", "tile"), "seq", None),
        P("group", None),
        P("tile", "seq"),
        P("seq", "tile"),
        P(),
        P(("group", "tile"), "seq", None),
        P(("group", "tile"), "seq"),
        P("group"),
    )
    out_specs = (P(("group", "tile"), "seq", None), P(("group", "tile"), "seq", None))
    return jax.shard_map(shards, mesh=mesh, in_specs=in_specs, out_specs=out_specs, check_vma=False)
```

time: 438 us -> 335 us (0.76)
  waiting for transfers between devices: 319 us -> 24.3 us
  Pallas kernels: 0 us -> 201 us
  local copies, waits for them, and re-layouts: 9.9 us -> 38.6 us
  starting transfers between devices: 24.8 us -> 7.81 us
  between operations: 14.9 us -> 1.63 us
  other arithmetic: 16.9 us -> 12.2 us
    all_gather x3 -> x0, waiting for transfers between devices: 205 us -> none  [the longest x1 115 us: shards(): gathered = lax.all_gather(norm_in, 'seq', axis=0, tiled=True)]
    pallas_call x0 -> x1, Pallas kernels: none -> 201 us  [gather(): pl.pallas_call(functools.partial(gather_kernel, groups, chips, seqs), out...]
    reduce_scatter x1 -> x0, waiting for transfers between devices: 111 us -> none  [shards(): lax.psum_scatter(jnp.dot(attended, full_out, preferred_element_type=jnp.f...]
    ppermute x8 -> x2, starting transfers between devices: 24.6 us -> 4.09 us  [the longest x1 2.17 us: shards(): lax.ppermute(weight.astype(jnp.bfloat16), ('tile', 'seq'), moves)]
    all_to_all x0 -> x1, waiting for transfers between devices: none -> 19.4 us  [shards(): lax.all_to_all(attended, 'seq', split_axis=0, concat_axis=1, tiled=True)]
    dot_general x0 -> x1, local copies, waits for them, and re-layouts: none -> 18.6 us  [shards(): jnp.dot(gathered, columns.reshape(-1, columns.shape[2]), preferred_elemen...]
    slice x1, local copies, waits for them, and re-layouts: 2.05 us -> 14.2 us  [shards(): out_blocks[at]]
    unnamed x25 -> x16, local copies, waits for them, and re-layouts: 7.19 us -> 0.07 us
  transfers between devices with their start and end apart: 12 -> 3, of which waited for: 5 -> 2; matrix products, arithmetic and copies ran while one was open for 12% -> 9% of each run, Pallas kernels for 0% -> 0%
where the time goes in v1:
time: 335 us; the launch traced here: 334 us
  Pallas kernels  201 us (60%)
  matrix products  48.8 us (15%)
  local copies, waits for them, and re-layouts  38.6 us (12%)
  waiting for transfers between devices  24.3 us (7%)
  other arithmetic  12.2 us (4%)
  starting transfers between devices  7.81 us (2%)
    pallas_call x1, Pallas kernels, gather(): pl.pallas_call(functools.partial(gather_kernel, groups, chips, seqs), out...  201 us
    dot_general x1, matrix products, shards(): jnp.dot(gathered, columns.reshape(-1, columns.shape[2]), preferred_elemen...  19.4 us
    all_to_all x1, waiting for transfers between devices, shards(): lax.all_to_all(attended, 'seq', split_axis=0, concat_axis=1, tiled=True)  19.4 us
    dot_general x1, local copies, waits for them, and re-layouts, shards(): jnp.dot(gathered, columns.reshape(-1, columns.shape[2]), preferred_elemen...  18.6 us
    slice x1, local copies, waits for them, and re-layouts, shards(): out_blocks[at]  14.2 us
    dot_general x4, matrix products, shards(): jnp.dot(attended, out_blocks[at], preferred_element_type=jnp.float32)  10.7 us
    dot_general x2, matrix products, shards(): jnp.einsum('hqk,khe->qhe', probs, values, preferred_element_type=jnp.floa...  8.92 us
    dot_general x2, matrix products, shards(): jnp.einsum('qhe,khe->hqk', queries[first:first + block], keys, preferred_...  8.71 us
  transfers between devices with their start and end apart: 3, of which 2 were waited for; matrix products, arithmetic and copies ran while one was open for 9% of the time, Pallas kernels for 0%

profile of v1, /device:TPU:2, one launch (start us, length us, event | category | flops | bytes accessed | tf_op | source)
XLA Modules:
  0.0 334.4 jit_solution(13058718854592547865)
XLA Ops:
  0.6 0.0 copy-start
  0.6 0.0 copy-start.1
  0.7 1.9 fusion.30
  2.5 1.7 convert_reduce_fusion
  4.3 2.0 fusion.8
  6.2 0.0 copy-done.1
  6.2 1.9 fusion.11.norm
  8.2 201.1 %shard_map.95 = (bf16[4,256,3072]{2,1,0:T(8,128)(2,1)}, bf16[4,768,2304]{2,1,0:T(8,128)(2,1)}, bf16[4,4,768,768]{3,2,1,0:T(8,128)(2,1)}) custom-call(bf16[256,3072]{1,0:T(8,128)(2,1)} %fusion.11.norm, bf16[768,2304]{1,0:T(8,128)(2,1)} %wq.1, bf16[768,768]{1,0:T(8,128)(2,1)} %wo.1), custom_call_target="tpu_custom_call" | custom-call | tf_op jit(solution)/shard_map/pallas_call | solution.py:217
  209.3 18.6 %copy.15 = bf16[2304,3072]{1,0:T(8,128)(2,1)} copy(bf16[2304,3072]{0,1:T(8,128)(2,1)} %bitcast.97) | data formatting | bytes 28311552 | tf_op jit(solution)/shard_map/dot_general | solution.py:240
  227.9 19.4 %fusion.31 = f32[1024,6,3,128]{0,3,2,1:T(8,128)S(1)} fusion(bf16[1024,3072,1,1]{1,0,3,2:T(8,128)(2,1)} %bitcast.120, bf16[6,3,128,3072]{3,2,1,0:T(8,128)(2,1)} %bitcast.98), kind=kOutput, calls=%fused_computation.60 | convolution fusion | flops 14495514624 | bytes 29884416 | tf_op jit(solution)/shard_map/dot_general | solution.py:240
  247.3 0.8 multiply_reduce_fusion.1
  248.2 0.4 multiply_convert_fusion.1
  248.7 5.9 %fusion = (f32[6,512]{1,0:T(8,128)S(1)}, f32[6,512,1024]{2,1,0:T(8,128)}) fusion(f32[1024,6,3,128]{0,3,2,1:T(8,128)S(1)} %fusion.31, f32[1024,6]{0,1:T(8,128)S(1)} %get-tuple-element.27, bf16[1024,6,128]{0,2,1:T(8,128)(2,1)S(1)} %multiply_convert_fusion.1), kind=kOutput, calls=%fused_computation.4 | convolution fusion | flops 813167616 | bytes 16560128 | tf_op jit(solution)/shard_map/qhe,khe->hqk/dot_general | solution.py:252
  254.6 2.8 fusion.1
  257.4 6.0 %fusion.16 = bf16[512,6,128]{0,2,1:T(8,128)(2,1)S(1)} fusion(f32[6,512,1024]{2,1,0:T(8,128)} %get-tuple-element.26, f32[6,512]{1,0:T(8,128)S(1)} %get-tuple-element.25, f32[1024,6,3,128]{0,3,2,1:T(8,128)S(1)} %fusion.31), kind=kOutput, calls=%fused_computation.33 | convolution fusion | flops 815136768 | bytes 14958592 | tf_op jit(solution)/shard_map/hqk,khe->qhe/dot_general | solution.py:263
  263.4 2.9 fusion.17
  266.3 0.2 pad_maximum_fusion
  266.5 2.4 all_to_all.14
  268.9 2.8 copy.20
  271.6 3.7 %all-to-all-start = ((bf16[4,256,768]{1,2,0:T(8,128)(2,1)}), bf16[4,256,768]{1,2,0:T(8,128)(2,1)S(1)}, u32[]{:S(2)}, u32[]{:S(2)}) async-start(bf16[4,256,768]{1,2,0:T(8,128)(2,1)} %copy.20), calls=%async_computation | async-start | bytes 3145728 | tf_op jit(solution)/shard_map/all_to_all | solution.py:268
  275.4 0.7 convert_element_type.80
  276.0 0.5 convert_element_type.84
  276.6 2.2 collective-permute-start.1
  279.5 14.2 %fusion.29 = (bf16[1,4,768,768]{3,2,1,0:T(8,128)(2,1)}, bf16[1,4,768,768]{3,2,1,0:T(8,128)(2,1)}, bf16[1,4,768,768]{3,2,1,0:T(8,128)(2,1)}, bf16[1,4,768,768]{3,2,1,0:T(8,128)(2,1)}) fusion(bf16[4,4,768,768]{3,2,1,0:T(8,128)(2,1)} %get-tuple-element.7), kind=kLoop, calls=%fused_computation.58 | loop fusion | bytes 37748736 | tf_op jit(solution)/shard_map/slice | solution.py:272
  293.7 19.4 %all-to-all-done = bf16[4,256,768]{1,2,0:T(8,128)(2,1)S(1)} async-done(((bf16[4,256,768]{1,2,0:T(8,128)(2,1)}), bf16[4,256,768]{1,2,0:T(8,128)(2,1)S(1)}, u32[]{:S(2)}, u32[]{:S(2)}) %all-to-all-start) | async-done | bytes 1572896 | tf_op jit(solution)/shard_map/all_to_all | solution.py:268
  313.1 3.9 %fusion.32 = f32[256,768]{1,0:T(8,128)S(1)} fusion(bf16[256,3072]{0,1:T(8,128)(2,1)S(1)} %bitcast.105, bf16[3072,768]{1,0:T(8,128)(2,1)} %bitcast.104), kind=kOutput, calls=%fused_computation.61 | convolution fusion | flops 1207959552 | bytes 7077888 | tf_op jit(solution)/shard_map/dot_general | solution.py:272
  317.0 0.0 slice-start
  317.0 3.9 %fusion.33 = f32[256,768]{1,0:T(8,128)S(1)} fusion(bf16[256,3072]{0,1:T(8,128)(2,1)S(1)} %bitcast.106, bf16[3072,768]{1,0:T(8,128)(2,1)} %bitcast.103), kind=kOutput, calls=%fused_computation.62 | convolution fusion | flops 1207959552 | bytes 7077888 | tf_op jit(solution)/shard_map/dot_general | solution.py:272
  320.9 0.0 copy-done.2
  320.9 0.0 slice-start.1
  320.9 1.4 fusion.34
  322.4 0.0 slice-done
  322.4 0.0 slice-done.1
  322.4 1.4 fusion.35
  323.8 0.5 fusion.28
  324.4 0.0 copy-start.4
  324.4 0.0 copy-start.5
  324.4 0.8 multiply_reduce_fusion
  325.2 0.0 copy-done
  325.2 0.0 copy-done.3
  325.2 0.0 copy-done.4
  325.2 0.0 copy-done.5
  325.3 1.0 bitcast_add_fusion
  326.3 1.9 collective-permute-start
  328.2 0.0 collective-permute-done.1
  328.3 0.6 convert_add_fusion
  328.9 4.8 %collective-permute-done = bf16[256,128]{0,1:T(8,128)(2,1)S(1)} collective-permute-done((bf16[256,128]{0,1:T(8,128)(2,1)S(1)}, bf16[256,128]{0,1:T(8,128)(2,1)S(1)}, u32[]{:S(2)}, u32[]{:S(2)}) %collective-permute-start) | collective-permute-done | bytes 65568 | tf_op jit(solution)/shard_map/ppermute | solution.py:296
  333.7 0.7 slice_bitcast_fusion.2
  (10 shorter events, 0.1 us)
Async XLA Ops:
  0.6 324.6 %copy-start = (bf16[3072,64]{0,1:T(8,128)(2,1)S(1)}, bf16[3072,64]{0,1:T(8,128)(2,1)}, u32[]{:S(2)}) copy-start(bf16[3072,64]{0,1:T(8,128)(2,1)} %param.12) | copy-start | bytes 1179652
  0.6 5.6 %copy-start.1 = (bf16[1,256,3072]{2,1,0:T(8,128)(2,1)S(1)}, bf16[1,256,3072]{2,1,0:T(8,128)(2,1)}, u32[]{:S(2)}) copy-start(bf16[1,256,3072]{2,1,0:T(8,128)(2,1)} %param.8) | copy-start | bytes 4718596
  271.6 41.5 %all-to-all-start = ((bf16[4,256,768]{1,2,0:T(8,128)(2,1)}), bf16[4,256,768]{1,2,0:T(8,128)(2,1)S(1)}, u32[]{:S(2)}, u32[]{:S(2)}) async-start(bf16[4,256,768]{1,2,0:T(8,128)(2,1)} %copy.20), calls=%async_computation | async-start | bytes 3145728 | tf_op jit(solution)/shard_map/all_to_all | solution.py:268
  276.6 51.7 %collective-permute-start.1 = (bf16[256]{0:T(256)(128)(2,1)}, bf16[256]{0:T(256)(128)(2,1)}, u32[]{:S(2)}, u32[]{:S(2)}) collective-permute-start(bf16[256]{0:T(256)(128)(2,1)} %convert_element_type.84), channel_id=1, source_target_pairs={{2,4},{3,5},{6,8},{7,9},{10,12},{11,13},{4,2},{5,3},{8,6},{9,7},{1... | collective-permute-start | bytes 1544 | tf_op jit(solution)/shard_map/ppermute | solution.py:297
  313.1 7.8 %copy-start.2 = (bf16[1,4,768,768]{3,2,1,0:T(8,128)(2,1)S(1)}, bf16[1,4,768,768]{3,2,1,0:T(8,128)(2,1)}, u32[]{:S(2)}) copy-start(bf16[1,4,768,768]{3,2,1,0:T(8,128)(2,1)} %get-tuple-element.12) | copy-start | bytes 14155780
  317.0 5.4 %slice-start = ((s8[4718592]{0:T(1024)(128)(4,1)}), s8[4194304]{0:T(1024)(128)(4,1)S(1)}, s32[]{:S(2)}) async-start(s8[4718592]{0:T(1024)(128)(4,1)} %bitcast.99), calls=%async_computation.1 | async-start | bytes 8388608
  320.9 1.5 slice-start.1
  324.4 0.8 copy-start.3
  324.4 0.8 copy-start.4
  324.4 0.9 copy-start.5
  326.3 7.4 %collective-permute-start = (bf16[256,128]{0,1:T(8,128)(2,1)S(1)}, bf16[256,128]{0,1:T(8,128)(2,1)S(1)}, u32[]{:S(2)}, u32[]{:S(2)}) collective-permute-start(bf16[256,128]{0,1:T(8,128)(2,1)S(1)} %fusion.24), channel_id=1, source_target_pairs={{2,4},{3,5},{6,8},{7,9},{10,12},{11,13},{4,2},{5,3},{8,6},{9,7},{1... | collective-permute-start | bytes 196616 | tf_op jit(solution)/shard_map/ppermute | solution.py:296

commit v2 on v1

--- a/solution.py
+++ b/solution.py
@@ -135,6 +135,25 @@
     for store in stores:
         store.start()
 
+    def rows_from_chips(rows):
+        for far in range(1, chips):
+            for way in (0, 1):
+                at = chip - far if way == 0 else chip + far
+                for given, row in rows:
+                    here = arrives(chip, chips, way, far)
+                    here = here if given is None else both(here, given)
+                    piece = o_part(at * 2 + core, row, group)
+                    arrived(here, piece, ox_s.at[way, far, row], ox_r.at[way, far, row], along_chip(way))
+                    if far < chips - 1:
+                        o_along_chip(both(here, goes_on(chip, chips, way)), way, far + 1, at, row, piece)
+                    o_to_peers(here, at, row, piece)
+                    o_to_partner(here, at, row, group, piece)
+
+    def rows_at(far):
+        if far == 0:
+            return [(None, place)]
+        return [(arrives(place, seqs, way, far), place - far if way == 0 else place + far) for way in (0, 1)]
+
     def seq_step(far):
         for way in (0, 1):
             here = arrives(place, seqs, way, far)
@@ -147,6 +166,8 @@
                 o_along_chip(both(here, goes_on(chip, chips, side)), side, 1, chip, row, piece)
             o_to_peers(here, chip, row, piece)
             o_to_partner(here, chip, row, group, piece)
+        if far > 1:
+            rows_from_chips(rows_at(far - 1))
         for way in (0, 1):
             here = arrives(place, seqs, way, far)
             row = place - far if way == 0 else place + far
@@ -171,19 +192,10 @@
             seq_step(far)
         if far < chips:
             chip_step(far)
-
-    for far in range(1, chips):
-        for way in (0, 1):
-            here = arrives(chip, chips, way, far)
-            at = chip - far if way == 0 else chip + far
-
-            for row in range(seqs):
-                piece = o_part(at * 2 + core, row, group)
-                arrived(here, piece, ox_s.at[way, far, row], ox_r.at[way, far, row], along_chip(way))
-                if far < chips - 1:
-                    o_along_chip(both(here, goes_on(chip, chips, way)), way, far + 1, at, row, piece)
-                o_to_peers(here, at, row, piece)
-                o_to_partner(here, at, row, group, piece)
+        if far == 1:
+            rows_from_chips(rows_at(0))
+    if seqs > 1:
+        rows_from_chips(rows_at(seqs - 1))
 
     for step in range(1, groups):
         part = (group + groups - step) % groups
@@ -230,53 +242,81 @@
     )(norm, wq, wo)
 
 
+def heads_kernel(scale, block, rows, weights, attended, queries, keys, values):
+    length = rows.shape[0]
+    for first in range(0, length, block):
+        at = pl.ds(first, block)
+        part = jnp.dot(rows[at, :], weights[...], preferred_element_type=jnp.float32)
+        queries[at, :] = root_norm(part[:, :HD]).astype(jnp.bfloat16)
+        keys[at, :] = root_norm(part[:, HD : 2 * HD]).astype(jnp.bfloat16)
+        values[at, :] = part[:, 2 * HD :].astype(jnp.bfloat16)
+    for first in range(0, length, block):
+        at = pl.ds(first, block)
+        scores = lax.dot_general(
+            queries[at, :], keys[...], (((1,), (1,)), ((), ())), preferred_element_type=jnp.float32
+        )
+        expo = jnp.exp(scores * scale)
+        probs = (expo * (1.0 / jnp.sum(expo, axis=-1, keepdims=True))).astype(jnp.bfloat16)
+        attended[at, :] = jnp.dot(probs, values[...], preferred_element_type=jnp.float32).astype(jnp.bfloat16)
+
+
+def attend(rows, weights):
+    length, width = rows.shape
+    heads = weights.shape[1] // (3 * HD)
+    return pl.pallas_call(
+        functools.partial(heads_kernel, 1.0 / math.sqrt(HD), min(256, length)),
+        grid=(heads,),
+        out_shape=jax.ShapeDtypeStruct((length, heads * HD), jnp.bfloat16),
+        in_specs=[
+            pl.BlockSpec((length, width), lambda head: (0, 0), pipeline_mode=pl.Buffered(1)),
+            pl.BlockSpec((width, 3 * HD), lambda head: (0, head)),
+        ],
+        out_specs=pl.BlockSpec((length, HD), lambda head: (0, head)),
+        scratch_shapes=[pltpu.VMEM((length, HD), jnp.bfloat16)] * 3,
+    )(rows, weights)
+
+
+def tail_kernel(attended, blocks, hidden, modulation, w_head, velocity, summed):
+    at = pl.program_id(0)
+    width = blocks.shape[2]
+    here = pl.ds(pl.multiple_of(at * width, 128), width)
+    summed[:, here] = jnp.dot(attended[...], blocks[0], preferred_element_type=jnp.float32)
+
+    @pl.when(at == pl.num_programs(0) - 1)
+    def _():
+        mixed = hidden[...].astype(jnp.float32) + modulation[2:3] * summed[...]
+        norm_out = (layer_norm(mixed) * (1.0 + modulation[4:5]) + modulation[3:4]).astype(jnp.bfloat16)
+        velocity[...] = jnp.dot(norm_out, w_head[...], preferred_element_type=jnp.float32)
+
+
+def tail(attended, blocks, hidden, modulation, w_head):
+    tiles, depth, width = blocks.shape
+    if width % 128:
+        summed = jnp.concatenate(
+            [jnp.dot(attended, blocks[at], preferred_element_type=jnp.float32) for at in range(tiles)], axis=1
+        )
+        mixed = hidden.astype(jnp.float32) + modulation[2] * summed
+        norm_out = (layer_norm(mixed) * (1.0 + modulation[4]) + modulation[3]).astype(jnp.bfloat16)
+        return jnp.dot(norm_out, w_head, preferred_element_type=jnp.float32)
+    whole = [pl.BlockSpec(a.shape, lambda at: (0, 0), pipeline_mode=pl.Buffered(1)) for a in (attended, hidden, modulation, w_head)]
+    return pl.pallas_call(
+        tail_kernel,
+        grid=(tiles,),
+        out_shape=jax.ShapeDtypeStruct((hidden.shape[0], w_head.shape[1]), jnp.float32),
+        in_specs=[whole[0], pl.BlockSpec((1, depth, width), lambda at: (at, 0, 0)), *whole[1:]],
+        out_specs=pl.BlockSpec((hidden.shape[0], w_head.shape[1]), lambda at: (0, 0)),
+        scratch_shapes=[pltpu.VMEM(hidden.shape, jnp.float32)],
+    )(attended, blocks, hidden, modulation, w_head)
+
+
 def shards(hidden, modulation, w_qkv, w_out, w_head, latent, weights_int, step_index):
     local = hidden[0].astype(jnp.float32)
     norm_in = (layer_norm(local) * (1.0 + modulation[1]) + modulation[0]).astype(jnp.bfloat16)
     rows, columns, out_blocks = gather(norm_in, w_qkv, w_out)
-    gathered = rows.reshape(-1, rows.shape[2])
-    length = gathered.shape[0]
-    heads_here = w_qkv.shape[1] // (3 * HD)
-    projected = jnp.dot(
-        gathered, columns.reshape(-1, columns.shape[2]), preferred_element_type=jnp.float32
-    )
-    projected = projected.reshape(length, heads_here, 3, HD)
-    queries = root_norm(projected[:, :, 0]).astype(jnp.bfloat16)
-    keys = root_norm(projected[:, :, 1]).astype(jnp.bfloat16)
-    values = projected[:, :, 2].astype(jnp.bfloat16)
-    block = min(512, length)
-    scale = 1.0 / math.sqrt(HD)
-    pieces = []
-    for first in range(0, length, block):
-        scores = (
-            jnp.einsum(
-                "qhe,khe->hqk",
-                queries[first : first + block],
-                keys,
-                preferred_element_type=jnp.float32,
-            )
-            * scale
-        )
-        expo = jnp.exp(scores)
-        probs = (expo / jnp.sum(expo, axis=-1, keepdims=True)).astype(jnp.bfloat16)
-        pieces.append(
-            jnp.einsum("hqk,khe->qhe", probs, values, preferred_element_type=jnp.float32).astype(
-                jnp.bfloat16
-            )
-        )
-    attended = jnp.concatenate(pieces, axis=0).reshape(length, heads_here * HD)
+    attended = attend(rows.reshape(-1, rows.shape[2]), columns.reshape(-1, columns.shape[2]))
     attended = lax.all_to_all(attended, "seq", split_axis=0, concat_axis=1, tiled=True)
     out_blocks = out_blocks.reshape(out_blocks.shape[0], -1, out_blocks.shape[3])
-    summed = jnp.concatenate(
-        [
-            jnp.dot(attended, out_blocks[at], preferred_element_type=jnp.float32)
-            for at in range(out_blocks.shape[0])
-        ],
-        axis=1,
-    )
-    mixed = local + modulation[2] * summed
-    norm_out = (layer_norm(mixed) * (1.0 + modulation[4]) + modulation[3]).astype(jnp.bfloat16)
-    velocity = jnp.dot(norm_out, w_head, preferred_element_type=jnp.float32)
+    velocity = tail(attended, out_blocks, hidden[0], modulation, w_head)
     index = step_index[0].astype(jnp.float32)
     now = noise_level(index, NSTEPS)
     after = noise_level(index + 1.0, NSTEPS)

time: 335 us -> 284 us (0.85)
  matrix products: 48.8 us -> 0 us
  local copies, waits for them, and re-layouts: 38.6 us -> 4.16 us
  Pallas kernels: 201 us -> 221 us
  waiting for transfers between devices: 24.3 us -> 39.2 us
  other arithmetic: 12.2 us -> 7.96 us
    pallas_call x0 -> x2, Pallas kernels: none -> 49.2 us  [the longest x1 36.7 us: attend(): pl.pallas_call(functools.partial(heads_kernel, 1.0 / math.sqrt(HD), min(2...]
    dot_general x10 -> x0, matrix products: 48.8 us -> none  [the longest x1 19.4 us: shards(): jnp.dot(gathered, columns.reshape(-1, columns.shape[2]), preferred_elemen...]
    pallas_call x1, Pallas kernels: 201 us -> 172 us  [gather(): pl.pallas_call(functools.partial(gather_kernel, groups, chips, seqs), out...]
    dot_general x1 -> x0, local copies, waits for them, and re-layouts: 18.6 us -> none  [shards(): jnp.dot(gathered, columns.reshape(-1, columns.shape[2]), preferred_elemen...]
    all_to_all x1, waiting for transfers between devices: 19.4 us -> 33.7 us  [shards(): lax.all_to_all(attended, 'seq', split_axis=0, concat_axis=1, tiled=True)]
    slice x1 -> x0, local copies, waits for them, and re-layouts: 14.2 us -> none  [shards(): out_blocks[at]]
    all_to_all x2 -> x1, local copies, waits for them, and re-layouts: 5.11 us -> 1.36 us  [shards(): lax.all_to_all(attended, 'seq', split_axis=0, concat_axis=1, tiled=True)]
  transfers between devices with their start and end apart: 3 -> 3, of which waited for: 2 -> 2; matrix products, arithmetic and copies ran while one was open for 9% -> 1% of each run, Pallas kernels for 0% -> 4%
where the time goes in v2:
time: 284 us
  Pallas kernels  221 us (78%)
  waiting for transfers between devices  39.2 us (14%)
  starting transfers between devices  10.2 us (4%)
  other arithmetic  7.96 us (3%)
  local copies, waits for them, and re-layouts  4.16 us (1%)
    pallas_call x1, Pallas kernels, gather(): pl.pallas_call(functools.partial(gather_kernel, groups, chips, seqs), out...  172 us
    pallas_call x1, Pallas kernels, attend(): pl.pallas_call(functools.partial(heads_kernel, 1.0 / math.sqrt(HD), min(2...  36.7 us
    all_to_all x1, waiting for transfers between devices, shards(): lax.all_to_all(attended, 'seq', split_axis=0, concat_axis=1, tiled=True)  33.7 us
    pallas_call x1, Pallas kernels, tail(): pl.pallas_call(tail_kernel, grid=(tiles,), out_shape=jax.ShapeDtypeStruct...  12.5 us
    all_to_all x1, starting transfers between devices, shards(): lax.all_to_all(attended, 'seq', split_axis=0, concat_axis=1, tiled=True)  6.38 us
  transfers between devices with their start and end apart: 3, of which 2 were waited for; matrix products, arithmetic and copies ran while one was open for 1% of the time, Pallas kernels for 4%

profile of v2, /device:TPU:2, one launch (start us, length us, event | category | flops | bytes accessed | tf_op | source)
XLA Modules:
  0.0 283.8 jit_solution(8974674324869102684)
XLA Ops:
  0.6 0.0 copy-start
  0.6 1.1 slice_add_fusion
  1.7 1.7 convert_reduce_fusion
  3.4 2.0 fusion.2
  5.4 0.0 copy-done
  5.4 2.0 fusion.5.norm
  7.4 171.6 %shard_map.95 = (bf16[4,256,3072]{2,1,0:T(8,128)(2,1)}, bf16[4,768,2304]{2,1,0:T(8,128)(2,1)}, bf16[4,4,768,768]{3,2,1,0:T(8,128)(2,1)}) custom-call(bf16[256,3072]{1,0:T(8,128)(2,1)} %fusion.5.norm, bf16[768,2304]{1,0:T(8,128)(2,1)} %wq.1, bf16[768,768]{1,0:T(8,128)(2,1)} %wo.1), custom_call_target="tpu_custom_call" | custom-call | tf_op jit(solution)/shard_map/pallas_call | solution.py:229
  179.0 36.7 %shard_map.96 = bf16[1024,768]{1,0:T(8,128)(2,1)} custom-call(bf16[1024,3072]{1,0:T(8,128)(2,1)} %bitcast.28, bf16[3072,2304]{1,0:T(8,128)(2,1)} %bitcast.25), custom_call_target="tpu_custom_call" | custom-call | tf_op jit(solution)/shard_map/pallas_call | solution.py:266
  215.7 0.0 copy-start.3
  215.7 0.0 copy-start.1
  215.7 0.0 copy-start.2
  215.7 6.4 %all-to-all-start = ((bf16[4,256,768]{2,1,0:T(8,128)(2,1)}), bf16[4,256,768]{2,1,0:T(8,128)(2,1)S(1)}, u32[]{:S(2)}, u32[]{:S(2)}) async-start(bf16[4,256,768]{2,1,0:T(8,128)(2,1)} %bitcast.29), calls=%async_computation | async-start | bytes 3145728 | tf_op jit(solution)/shard_map/all_to_all | solution.py:317
  222.1 0.0 copy-done.3
  222.1 1.9 collective-permute-start.1
  224.7 0.0 copy-done.1
  224.7 1.2 copy.17.w_head
  225.8 0.0 copy-done.2
  225.8 0.1 copy.15
  226.0 33.7 %all-to-all-done = bf16[4,256,768]{2,1,0:T(8,128)(2,1)S(1)} async-done(((bf16[4,256,768]{2,1,0:T(8,128)(2,1)}), bf16[4,256,768]{2,1,0:T(8,128)(2,1)S(1)}, u32[]{:S(2)}, u32[]{:S(2)}) %all-to-all-start) | async-done | bytes 1572896 | tf_op jit(solution)/shard_map/all_to_all | solution.py:317
  259.7 1.4 copy.20
  261.1 12.5 %shard_map.97 = f32[256,64]{1,0:T(8,128)} custom-call(bf16[256,3072]{1,0:T(8,128)(2,1)} %bitcast.27, bf16[4,3072,768]{2,1,0:T(8,128)(2,1)} %bitcast.24, bf16[256,3072]{1,0:T(8,128)(2,1)} %bitcast.23, f32[5,3072]{1,0:T(8,128)} %modulation.1, bf16[3072,64]{1,0:T(8,128)(2,1)} %copy.17.w_head), custom_call_target="tpu_custom_call" | custom-call | tf_op jit(solution)/shard_map/pallas_call | solution.py:302
  273.6 0.9 bitcast_add_fusion
  274.5 0.1 fusion.6
  274.7 1.9 collective-permute-start
  276.6 0.0 collective-permute-done.1
  276.6 5.4 %collective-permute-done = bf16[256,128]{1,0:T(8,128)(2,1)S(1)} collective-permute-done((bf16[256,128]{1,0:T(8,128)(2,1)S(1)}, bf16[256,128]{1,0:T(8,128)(2,1)S(1)}, u32[]{:S(2)}, u32[]{:S(2)}) %collective-permute-start) | collective-permute-done | bytes 65568 | tf_op jit(solution)/shard_map/ppermute | solution.py:336
  282.1 0.2 add_divide_fusion
  282.3 0.1 slice_bitcast_fusion
  282.3 0.7 copy.18
  283.1 0.7 copy.19
  (5 shorter events, 0.0 us)
Async XLA Ops:
  0.6 4.8 %copy-start = (bf16[1,256,3072]{2,1,0:T(8,128)(2,1)S(1)}, bf16[1,256,3072]{2,1,0:T(8,128)(2,1)}, u32[]{:S(2)}) copy-start(bf16[1,256,3072]{2,1,0:T(8,128)(2,1)} %param.8) | copy-start | bytes 4718596
  215.7 6.4 %copy-start.3 = (s32[1,256]{1,0:T(1,128)S(1)}, s32[1,256]{1,0:T(1,128)}, u32[]{:S(2)}) copy-start(s32[1,256]{1,0:T(1,128)} %param.14) | copy-start | bytes 3076
  215.7 9.0 %copy-start.1 = (bf16[3072,64]{0,1:T(8,128)(2,1)S(1)}, bf16[3072,64]{0,1:T(8,128)(2,1)}, u32[]{:S(2)}) copy-start(bf16[3072,64]{0,1:T(8,128)(2,1)} %param.12) | copy-start | bytes 1179652
  215.7 10.2 %copy-start.2 = (f32[1,256,64]{1,2,0:T(8,128)S(1)}, f32[1,256,64]{1,2,0:T(8,128)}, u32[]{:S(2)}) copy-start(f32[1,256,64]{1,2,0:T(8,128)} %param.13) | copy-start | bytes 196612
  215.7 44.1 %all-to-all-start = ((bf16[4,256,768]{2,1,0:T(8,128)(2,1)}), bf16[4,256,768]{2,1,0:T(8,128)(2,1)S(1)}, u32[]{:S(2)}, u32[]{:S(2)}) async-start(bf16[4,256,768]{2,1,0:T(8,128)(2,1)} %bitcast.29), calls=%async_computation | async-start | bytes 3145728 | tf_op jit(solution)/shard_map/all_to_all | solution.py:317
  222.1 54.5 %collective-permute-start.1 = (bf16[256]{0:T(256)(128)(2,1)S(1)}, bf16[256]{0:T(256)(128)(2,1)S(1)}, u32[]{:S(2)}, u32[]{:S(2)}) collective-permute-start(bf16[256]{0:T(256)(128)(2,1)S(1)} %convert_element_type.39), channel_id=1, source_target_pairs={{2,4},{3,5},{6,8},{7,9},{10,12},{11,13},{4,2},{5,3},{8,6},{9,7},{1... | collective-permute-start | bytes 1544 | tf_op jit(solution)/shard_map/ppermute | solution.py:337
  274.7 7.4 %collective-permute-start = (bf16[256,128]{1,0:T(8,128)(2,1)S(1)}, bf16[256,128]{1,0:T(8,128)(2,1)S(1)}, u32[]{:S(2)}, u32[]{:S(2)}) collective-permute-start(bf16[256,128]{1,0:T(8,128)(2,1)S(1)} %fusion.6), channel_id=1, source_target_pairs={{2,4},{3,5},{6,8},{7,9},{10,12},{11,13},{4,2},{5,3},{8,6},{9,7},{1... | collective-permute-start | bytes 196616 | tf_op jit(solution)/shard_map/ppermute | solution.py:336

commit v3 on v2

--- a/solution.py
+++ b/solution.py
@@ -47,7 +47,8 @@
 
 
 def gather_kernel(
-    groups, chips, seqs, norm, wq, wo, n_all, q_all, o_all, v_norm, v_wq, v_wo, local,
+    groups, chips, seqs, scale, norm, wq, wo, q_all, o_all, attended,
+    n_all, v_wq, v_wo, w_head, queries, keys, values, local, w_sem,
     nz_s, nz_r, oz_s, oz_r, qx_s, qx_r, ox_s, ox_r, qy_s, qy_r, oy_s, oy_r, qc_s, qc_r, oc_s, oc_r,
 ):
     group, tile, place = lax.axis_index("group"), lax.axis_index("tile"), lax.axis_index("seq")
@@ -112,7 +113,7 @@
     def o_along_chip(cond, way, far, at, row, source):
         start(cond, source, o_part(at * 2 + core, row, group), ox_s.at[way, far, row], ox_r.at[way, far, row], along_chip(way))
 
-    loads = [pltpu.make_async_copy(a, b, local.at[k]) for k, (a, b) in enumerate(((norm, v_norm), (wq, v_wq), (wo, v_wo)))]
+    loads = [pltpu.make_async_copy(a, b, local.at[k]) for k, (a, b) in enumerate(((norm, n_all.at[place]), (wq, v_wq), (wo, v_wo)))]
     for load in loads:
         load.start()
 
@@ -120,8 +121,8 @@
     own_o = wo.at[pl.ds(pl.multiple_of(group * o_rows, 8), o_rows)]
     for way in (0, 1):
         go = goes_on(place, seqs, way)
+        start(go, norm, n_all.at[place], nz_s.at[way, 1], nz_r.at[way, 1], along_seq(way))
         start(go, own_o, o_part(tile, place, group), oz_s.at[way, 1], oz_r.at[way, 1], along_seq(way))
-        start(go, norm, n_all.at[place], nz_s.at[way, 1], nz_r.at[way, 1], along_seq(way))
         go = goes_on(chip, chips, way)
         start(go, own_q, q_part(tile, group), qx_s.at[way, 1], qx_r.at[way, 1], along_chip(way))
         o_along_chip(go, way, 1, chip, place, own_o)
@@ -129,7 +130,7 @@
         q_to_partner(None, chip, part, wq.at[pl.ds(part * q_rows, q_rows)])
         o_to_partner(None, chip, place, part, wo.at[pl.ds(part * o_rows, o_rows)])
 
-    stores = [pltpu.make_async_copy(b, a, local.at[k]) for k, (a, b) in enumerate(((n_all.at[place], v_norm), (q_all.at[tile], v_wq), (o_all.at[tile, place], v_wo)))]
+    stores = [pltpu.make_async_copy(b, a, local.at[k]) for k, (a, b) in enumerate(((q_all.at[tile], v_wq), (o_all.at[tile, place], v_wo)))]
     for load in loads:
         load.wait()
     for store in stores:
@@ -154,7 +155,7 @@
             return [(None, place)]
         return [(arrives(place, seqs, way, far), place - far if way == 0 else place + far) for way in (0, 1)]
 
-    def seq_step(far):
+    def out_step(far):
         for way in (0, 1):
             here = arrives(place, seqs, way, far)
             row = place - far if way == 0 else place + far
@@ -166,8 +167,8 @@
                 o_along_chip(both(here, goes_on(chip, chips, side)), side, 1, chip, row, piece)
             o_to_peers(here, chip, row, piece)
             o_to_partner(here, chip, row, group, piece)
-        if far > 1:
-            rows_from_chips(rows_at(far - 1))
+
+    def norm_step(far):
         for way in (0, 1):
             here = arrives(place, seqs, way, far)
             row = place - far if way == 0 else place + far
@@ -187,93 +188,132 @@
             q_to_peers(here, at, piece)
             q_to_partner(here, at, group, piece)
 
-    for far in range(1, max(chips, seqs)):
+    def q_from_peers():
+        for step in range(1, groups):
+            part = (group + groups - step) % groups
+            for at in range(chips):
+                away = chip != at
+                piece = q_part(at * 2 + core, part)
+                arrived(away, piece, qy_s.at[at, step], qy_r.at[at, step], partner)
+                q_to_partner(away, at, part, piece)
+
+    def o_from_peers():
+        for step in range(1, groups):
+            part = (group + groups - step) % groups
+            for at in range(chips):
+                for row in range(seqs):
+                    away = jnp.logical_or(chip != at, place != row)
+                    piece = o_part(at * 2 + core, row, part)
+                    arrived(away, piece, oy_s.at[at, row, step], oy_r.at[at, row, step], partner)
+                    o_to_partner(away, at, row, part, piece)
+
+    last = max(chips, seqs) - 1
+    for far in range(1, last + 1):
+        if 1 < far < seqs:
+            rows_from_chips(rows_at(far - 1))
         if far < seqs:
-            seq_step(far)
+            norm_step(far)
+        if far < seqs - 1:
+            out_step(far)
         if far < chips:
             chip_step(far)
-        if far == 1:
+        if far == 1 and seqs > 1:
             rows_from_chips(rows_at(0))
-    if seqs > 1:
-        rows_from_chips(rows_at(seqs - 1))
-
-    for step in range(1, groups):
-        part = (group + groups - step) % groups
-        for at in range(chips):
-            away = chip != at
-            piece = q_part(at * 2 + core, part)
-            arrived(away, piece, qy_s.at[at, step], qy_r.at[at, step], partner)
-            q_to_partner(away, at, part, piece)
-        for at in range(chips):
-            for row in range(seqs):
-                away = jnp.logical_or(chip != at, place != row)
-                piece = o_part(at * 2 + core, row, part)
-                arrived(away, piece, oy_s.at[at, row, step], oy_r.at[at, row, step], partner)
-                o_to_partner(away, at, row, part, piece)
-
+        if far == max(chips - 1, min(2, last)):
+            q_from_peers()
     for at in range(chips):
         for part in range(groups):
             arrived(None, q_part(at * 2 + other, part), qc_s.at[at, part], qc_r.at[at, part], partner)
+    for store in stores:
+        store.wait()
+
+    heads = wq.shape[1] // (3 * HD)
+    depth, block = wq.shape[0], norm.shape[0]
+
+    def fetch(head):
+        slot = head % 2
+        columns = pl.ds(pl.multiple_of(head * (3 * HD), 128), 3 * HD)
+        return [
+            pltpu.make_async_copy(
+                q_all.at[at, :, columns], w_head.at[slot, pl.ds(at * depth, depth)], w_sem.at[slot, at]
+            )
+            for at in range(2 * chips)
+        ]
+
+    def one_head(head, carry):
+        for load in fetch(head):
+            load.wait()
+
+        @pl.when(head + 1 < heads)
+        def _():
+            for load in fetch(head + 1):
+                load.start()
+
+        weights = w_head.at[head % 2]
+        for row in range(seqs):
+            at = pl.ds(row * block, block)
+            part = jnp.dot(n_all[row], weights[...], preferred_element_type=jnp.float32)
+            queries[at, :] = root_norm(part[:, :HD]).astype(jnp.bfloat16)
+            keys[at, :] = root_norm(part[:, HD : 2 * HD]).astype(jnp.bfloat16)
+            values[at, :] = part[:, 2 * HD :].astype(jnp.bfloat16)
+        for row in range(seqs):
+            at = pl.ds(row * block, block)
+            scores = lax.dot_general(
+                queries[at, :], keys[...], (((1,), (1,)), ((), ())), preferred_element_type=jnp.float32
+            )
+            expo = jnp.exp(scores * scale)
+            probs = (expo * (1.0 / jnp.sum(expo, axis=-1, keepdims=True))).astype(jnp.bfloat16)
+            attended[at, pl.ds(pl.multiple_of(head * HD, 128), HD)] = jnp.dot(
+                probs, values[...], preferred_element_type=jnp.float32
+            ).astype(jnp.bfloat16)
+        return carry
+
+    def between(step):
+        if step == 0 and seqs > 1:
+            out_step(seqs - 1)
+        if step == 1:
+            rows_from_chips(rows_at(seqs - 1))
+        if step == 2:
+            o_from_peers()
+
+    for load in fetch(0):
+        load.start()
+    cuts = [0, heads // 3, heads // 2, 5 * heads // 6, heads]
+    for step in range(4):
+        if cuts[step] < cuts[step + 1]:
+            lax.fori_loop(cuts[step], cuts[step + 1], one_head, 0)
+        between(step)
+
+    for at in range(chips):
+        for part in range(groups):
             for row in range(seqs):
                 arrived(None, o_part(at * 2 + other, row, part), oc_s.at[at, row, part], oc_r.at[at, row, part], partner)
     for cond, made in sent:
         run(cond, lambda made=made: copy(*made).wait_send())
-    for store in stores:
-        store.wait()
 
 
 def gather(norm, wq, wo):
     groups, tiles, seqs = (lax.axis_size(name) for name in ("group", "tile", "seq"))
     chips = tiles // 2
+    length = seqs * norm.shape[0]
     pairs = [(2, seqs), (2, seqs), (2, chips), (2, chips, seqs), (chips, groups), (chips, seqs, groups), (chips, groups), (chips, seqs, groups)]
     return pl.pallas_call(
-        functools.partial(gather_kernel, groups, chips, seqs),
+        functools.partial(gather_kernel, groups, chips, seqs, 1.0 / math.sqrt(HD)),
         out_shape=(
-            jax.ShapeDtypeStruct((seqs,) + norm.shape, norm.dtype),
             jax.ShapeDtypeStruct((tiles,) + wq.shape, wq.dtype),
             jax.ShapeDtypeStruct((tiles, seqs) + wo.shape, wo.dtype),
+            jax.ShapeDtypeStruct((length, wq.shape[1] // 3), norm.dtype),
         ),
         in_specs=[pl.BlockSpec(memory_space=pl.ANY)] * 3,
-        out_specs=(pl.BlockSpec(memory_space=pl.ANY),) * 3,
-        scratch_shapes=[pltpu.VMEM(a.shape, a.dtype) for a in (norm, wq, wo)]
-        + [pltpu.SemaphoreType.DMA((3,))]
+        out_specs=(pl.BlockSpec(memory_space=pl.ANY),) * 2 + (pl.BlockSpec(memory_space=pltpu.VMEM),),
+        scratch_shapes=[pltpu.VMEM((seqs,) + norm.shape, norm.dtype)]
+        + [pltpu.VMEM(a.shape, a.dtype) for a in (wq, wo)]
+        + [pltpu.VMEM((2, tiles * wq.shape[0], 3 * HD), wq.dtype)]
+        + [pltpu.VMEM((length, HD), norm.dtype)] * 3
+        + [pltpu.SemaphoreType.DMA((3,)), pltpu.SemaphoreType.DMA((2, tiles))]
         + [pltpu.SemaphoreType.DMA(shape) for shape in pairs for _ in range(2)],
         compiler_params=pltpu.CompilerParams(collective_id=0, has_side_effects=True),
     )(norm, wq, wo)
-
-
-def heads_kernel(scale, block, rows, weights, attended, queries, keys, values):
-    length = rows.shape[0]
-    for first in range(0, length, block):
-        at = pl.ds(first, block)
-        part = jnp.dot(rows[at, :], weights[...], preferred_element_type=jnp.float32)
-        queries[at, :] = root_norm(part[:, :HD]).astype(jnp.bfloat16)
-        keys[at, :] = root_norm(part[:, HD : 2 * HD]).astype(jnp.bfloat16)
-        values[at, :] = part[:, 2 * HD :].astype(jnp.bfloat16)
-    for first in range(0, length, block):
-        at = pl.ds(first, block)
-        scores = lax.dot_general(
-            queries[at, :], keys[...], (((1,), (1,)), ((), ())), preferred_element_type=jnp.float32
-        )
-        expo = jnp.exp(scores * scale)
-        probs = (expo * (1.0 / jnp.sum(expo, axis=-1, keepdims=True))).astype(jnp.bfloat16)
-        attended[at, :] = jnp.dot(probs, values[...], preferred_element_type=jnp.float32).astype(jnp.bfloat16)
-
-
-def attend(rows, weights):
-    length, width = rows.shape
-    heads = weights.shape[1] // (3 * HD)
-    return pl.pallas_call(
-        functools.partial(heads_kernel, 1.0 / math.sqrt(HD), min(256, length)),
-        grid=(heads,),
-        out_shape=jax.ShapeDtypeStruct((length, heads * HD), jnp.bfloat16),
-        in_specs=[
-            pl.BlockSpec((length, width), lambda head: (0, 0), pipeline_mode=pl.Buffered(1)),
-            pl.BlockSpec((width, 3 * HD), lambda head: (0, head)),
-        ],
-        out_specs=pl.BlockSpec((length, HD), lambda head: (0, head)),
-        scratch_shapes=[pltpu.VMEM((length, HD), jnp.bfloat16)] * 3,
-    )(rows, weights)
 
 
 def tail_kernel(attended, blocks, hidden, modulation, w_head, velocity, summed):
@@ -312,8 +352,7 @@
 def shards(hidden, modulation, w_qkv, w_out, w_head, latent, weights_int, step_index):
     local = hidden[0].astype(jnp.float32)
     norm_in = (layer_norm(local) * (1.0 + modulation[1]) + modulation[0]).astype(jnp.bfloat16)
-    rows, columns, out_blocks = gather(norm_in, w_qkv, w_out)
-    attended = attend(rows.reshape(-1, rows.shape[2]), columns.reshape(-1, columns.shape[2]))
+    _, out_blocks, attended = gather(norm_in, w_qkv, w_out)
     attended = lax.all_to_all(attended, "seq", split_axis=0, concat_axis=1, tiled=True)
     out_blocks = out_blocks.reshape(out_blocks.shape[0], -1, out_blocks.shape[3])
     velocity = tail(attended, out_blocks, hidden[0], modulation, w_head)

time: 284 us -> 261 us (0.919)
  Pallas kernels: 221 us -> 199 us
    pallas_call x2 -> x1, Pallas kernels: 208 us -> 187 us  [gather(): pl.pallas_call(functools.partial(gather_kernel, groups, chips, seqs, 1.0...]
  transfers between devices with their start and end apart: 3 -> 3, of which waited for: 2 -> 2; matrix products, arithmetic and copies ran while one was open for 1% -> 1% of each run, Pallas kernels for 4% -> 5%
where the time goes in v3:
time: 261 us
  Pallas kernels  199 us (76%)
  waiting for transfers between devices  39.1 us (15%)
  starting transfers between devices  9.1 us (3%)
  other arithmetic  7.93 us (3%)
  local copies, waits for them, and re-layouts  4.17 us (2%)
    pallas_call x1, Pallas kernels, gather(): pl.pallas_call(functools.partial(gather_kernel, groups, chips, seqs, 1.0...  187 us
    all_to_all x1, waiting for transfers between devices, shards(): lax.all_to_all(attended, 'seq', split_axis=0, concat_axis=1, tiled=True)  33.7 us
    pallas_call x1, Pallas kernels, tail(): pl.pallas_call(tail_kernel, grid=(tiles,), out_shape=jax.ShapeDtypeStruct...  12.5 us
    ppermute x1, waiting for transfers between devices, shards(): lax.ppermute(weighted.astype(jnp.bfloat16), ('tile', 'seq'), moves)  5.43 us
    all_to_all x1, starting transfers between devices, shards(): lax.all_to_all(attended, 'seq', split_axis=0, concat_axis=1, tiled=True)  5.26 us
  transfers between devices with their start and end apart: 3, of which 2 were waited for; matrix products, arithmetic and copies ran while one was open for 1% of the time, Pallas kernels for 5%

profile of v3, /device:TPU:2, one launch (start us, length us, event | category | flops | bytes accessed | tf_op | source)
XLA Modules:
  0.0 261.0 jit_solution(18182251112621841405)
XLA Ops:
  0.6 0.0 copy-start
  0.6 1.1 slice_add_fusion
  1.7 1.7 convert_reduce_fusion
  3.4 2.0 fusion.2
  5.4 0.0 copy-done
  5.4 1.9 fusion.5.norm
  7.3 186.6 %shard_map.95 = (bf16[4,768,2304]{2,1,0:T(8,128)(2,1)}, bf16[4,4,768,768]{3,2,1,0:T(8,128)(2,1)}, bf16[1024,768]{1,0:T(8,128)(2,1)}) custom-call(bf16[256,3072]{1,0:T(8,128)(2,1)} %fusion.5.norm, bf16[768,2304]{1,0:T(8,128)(2,1)} %wq.1, bf16[768,768]{1,0:T(8,128)(2,1)} %wo.1), custom_call_target="tpu_custom_call" | custom-call | tf_op jit(solution)/shard_map/pallas_call | solution.py:300
  194.0 0.0 copy-start.3
  194.0 0.0 copy-start.1
  194.0 0.0 copy-start.2
  194.0 5.3 %all-to-all-start = ((bf16[4,256,768]{2,1,0:T(8,128)(2,1)}), bf16[4,256,768]{2,1,0:T(8,128)(2,1)S(1)}, u32[]{:S(2)}, u32[]{:S(2)}) async-start(bf16[4,256,768]{2,1,0:T(8,128)(2,1)} %bitcast.25), calls=%async_computation | async-start | bytes 3145728 | tf_op jit(solution)/shard_map/all_to_all | solution.py:356
  199.3 0.0 copy-done.3
  199.3 1.9 collective-permute-start.1
  201.9 0.0 copy-done.1
  201.9 1.2 copy.17.w_head
  203.0 0.0 copy-done.2
  203.0 0.1 copy.15
  203.2 33.7 %all-to-all-done = bf16[4,256,768]{2,1,0:T(8,128)(2,1)S(1)} async-done(((bf16[4,256,768]{2,1,0:T(8,128)(2,1)}), bf16[4,256,768]{2,1,0:T(8,128)(2,1)S(1)}, u32[]{:S(2)}, u32[]{:S(2)}) %all-to-all-start) | async-done | bytes 1572896 | tf_op jit(solution)/shard_map/all_to_all | solution.py:356
  236.9 1.4 copy.20
  238.3 12.5 %shard_map.96 = f32[256,64]{1,0:T(8,128)} custom-call(bf16[256,3072]{1,0:T(8,128)(2,1)} %bitcast.24, bf16[4,3072,768]{2,1,0:T(8,128)(2,1)} %bitcast.22, bf16[256,3072]{1,0:T(8,128)(2,1)} %bitcast.21, f32[5,3072]{1,0:T(8,128)} %modulation.1, bf16[3072,64]{1,0:T(8,128)(2,1)} %copy.17.w_head), custom_call_target="tpu_custom_call" | custom-call | tf_op jit(solution)/shard_map/pallas_call | solution.py:342
  250.8 0.9 bitcast_add_fusion
  251.7 0.1 fusion.6
  251.9 1.9 collective-permute-start
  253.8 0.0 collective-permute-done.1
  253.8 5.4 %collective-permute-done = bf16[256,128]{1,0:T(8,128)(2,1)S(1)} collective-permute-done((bf16[256,128]{1,0:T(8,128)(2,1)S(1)}, bf16[256,128]{1,0:T(8,128)(2,1)S(1)}, u32[]{:S(2)}, u32[]{:S(2)}) %collective-permute-start) | collective-permute-done | bytes 65568 | tf_op jit(solution)/shard_map/ppermute | solution.py:375
  259.3 0.2 add_divide_fusion
  259.4 0.1 slice_bitcast_fusion
  259.5 0.7 copy.18
  260.3 0.7 copy.19
  (5 shorter events, 0.0 us)
Async XLA Ops:
  0.6 4.8 %copy-start = (bf16[1,256,3072]{2,1,0:T(8,128)(2,1)S(1)}, bf16[1,256,3072]{2,1,0:T(8,128)(2,1)}, u32[]{:S(2)}) copy-start(bf16[1,256,3072]{2,1,0:T(8,128)(2,1)} %param.8) | copy-start | bytes 4718596
  194.0 5.3 %copy-start.3 = (s32[1,256]{1,0:T(1,128)S(1)}, s32[1,256]{1,0:T(1,128)}, u32[]{:S(2)}) copy-start(s32[1,256]{1,0:T(1,128)} %param.14) | copy-start | bytes 3076
  194.0 7.9 %copy-start.1 = (bf16[3072,64]{0,1:T(8,128)(2,1)S(1)}, bf16[3072,64]{0,1:T(8,128)(2,1)}, u32[]{:S(2)}) copy-start(bf16[3072,64]{0,1:T(8,128)(2,1)} %param.12) | copy-start | bytes 1179652
  194.0 9.0 %copy-start.2 = (f32[1,256,64]{1,2,0:T(8,128)S(1)}, f32[1,256,64]{1,2,0:T(8,128)}, u32[]{:S(2)}) copy-start(f32[1,256,64]{1,2,0:T(8,128)} %param.13) | copy-start | bytes 196612
  194.0 42.9 %all-to-all-start = ((bf16[4,256,768]{2,1,0:T(8,128)(2,1)}), bf16[4,256,768]{2,1,0:T(8,128)(2,1)S(1)}, u32[]{:S(2)}, u32[]{:S(2)}) async-start(bf16[4,256,768]{2,1,0:T(8,128)(2,1)} %bitcast.25), calls=%async_computation | async-start | bytes 3145728 | tf_op jit(solution)/shard_map/all_to_all | solution.py:356
  199.3 54.5 %collective-permute-start.1 = (bf16[256]{0:T(256)(128)(2,1)S(1)}, bf16[256]{0:T(256)(128)(2,1)S(1)}, u32[]{:S(2)}, u32[]{:S(2)}) collective-permute-start(bf16[256]{0:T(256)(128)(2,1)S(1)} %convert_element_type.39), channel_id=1, source_target_pairs={{2,4},{3,5},{6,8},{7,9},{10,12},{11,13},{4,2},{5,3},{8,6},{9,7},{1... | collective-permute-start | bytes 1544 | tf_op jit(solution)/shard_map/ppermute | solution.py:376
  251.9 7.4 %collective-permute-start = (bf16[256,128]{1,0:T(8,128)(2,1)S(1)}, bf16[256,128]{1,0:T(8,128)(2,1)S(1)}, u32[]{:S(2)}, u32[]{:S(2)}) collective-permute-start(bf16[256,128]{1,0:T(8,128)(2,1)S(1)} %fusion.6), channel_id=1, source_target_pairs={{2,4},{3,5},{6,8},{7,9},{10,12},{11,13},{4,2},{5,3},{8,6},{9,7},{1... | collective-permute-start | bytes 196616 | tf_op jit(solution)/shard_map/ppermute | solution.py:375
